TPU v7x, 32 devices: a whole 2x2x4 slice. The times are simulated.
32 devices in a mesh: rep: 4 (over z), col: 8 (over y, x, core).
Axes of the slice: x: 2, y: 2, z: 4, core: 2. Of those that a mesh axis runs over, the one named last changes fastest.
Arguments:
- acts: bfloat16 [8192, 4096], P('rep'), may hold values from -40 to 40
- cotangent: bfloat16 [8192, 8192], P('rep', 'col'), may hold values from -40 to 40
- weight: float32 [4096, 8192], P(('rep', 'col')), may hold values from -6 to 6
- moment: float32 [4096, 8192], P(('rep', 'col')), may hold values from -3 to 3
- second: float32 [4096, 8192], P(('rep', 'col')), may hold values from 0.25 to 4
Outputs:
- new_weight: float32 [4096, 8192], P(('rep', 'col'))
- new_moment: float32 [4096, 8192], P(('rep', 'col'))
- new_second: float32 [4096, 8192], P(('rep', 'col'))
- combined: float32 [4096, 8192], P(('rep', 'col'))
All inputs are finite; a program needn't handle non-finite values.
Results may differ from a plain program's by a relative error of at most 0.0003.
Values may be sent and summed in bfloat16 or wider, within the bound.
No kernel may reach another device: no remote copies, remote signals or barrier semaphores. Data moves between devices by JAX's collectives and lax.ppermute only.
A program may use at most 128 MiB of HBM per device.

v0:
```python
import jax
import jax.numpy as jnp
from jax import lax
from jax.sharding import PartitionSpec as P

bias_first = 0.9999734386011124
bias_second = 0.99407947077966


def swapped(block, axis, distance):
    count = lax.axis_size(axis)
    route = []
    for low in range(count):
        high = low | 1 << distance
        if high != low and high < count:
            route += [(low, high), (high, low)]
    return lax.ppermute(block, axis, route)


def split_half(segment, parity):
    folded = segment.reshape((segment.shape[0] // 2, 2) + segment.shape[1:])
    keeper = lax.dynamic_index_in_dim(folded, parity, 1, keepdims=False)
    giving = lax.dynamic_index_in_dim(folded, 1 - parity, 1, keepdims=False)
    return (keeper, giving)


def group_total(values, level):
    total = lax.psum(values, "col")
    for pairing in range(level + 1):
        total = total + swapped(total, "rep", pairing)
    return total


def halving_rows(acts, cotangent, replicas, levels, rep_rank):
    tokens_here, depth = acts.shape
    columns = cotangent.shape[1]
    block_rows = depth // replicas
    segment = None
    gradient = jnp.einsum("td,tc->dc", acts, cotangent, preferred_element_type=jnp.float32)
    segment = gradient.reshape(replicas, block_rows, columns)
    for level in range(levels):
        parity = rep_rank >> level & 1
        own_part, giving = split_half(segment, parity)
        peer_part = swapped(giving, "rep", level)
        own_sq = jnp.sum(own_part * own_part)
        peer_sq = jnp.sum(peer_part * peer_part)
        cross = jnp.sum(own_part * peer_part)
        lower_sq = jnp.where(parity == 0, own_sq, peer_sq)
        upper_sq = jnp.where(parity == 0, peer_sq, own_sq)
        totals = group_total(jnp.stack([lower_sq, upper_sq, cross]), level)
        own_total = jnp.where(parity == 0, totals[0], totals[1])
        peer_total = jnp.where(parity == 0, totals[1], totals[0])
        own_coef = 1.0 - totals[2] / (2.0 * (own_total + 1e-06))
        peer_coef = 1.0 - totals[2] / (2.0 * (peer_total + 1e-06))
        segment = own_coef * own_part + peer_coef * peer_part
    return segment.reshape(block_rows, columns)


def per_device(acts, cotangent, weight, moment, second):
    replicas = lax.axis_size("rep")
    levels = replicas.bit_length() - 1
    rep_rank = lax.axis_index("rep")
    reduced = halving_rows(acts, cotangent, replicas, levels, rep_rank)
    combined = lax.all_to_all(reduced, "col", split_axis=0, concat_axis=1, tiled=True)
    new_moment = 0.9 * moment + 0.1 * combined
    new_second = 0.95 * second + 0.05 * combined * combined
    update = new_moment / bias_first / (jnp.sqrt(new_second / bias_second) + 1e-08) + 0.1 * weight
    new_weight = weight - 0.0003 * update
    return (new_weight, new_moment, new_second, combined)


def solution(mesh):
    return jax.shard_map(
        per_device,
        mesh=mesh,
        in_specs=(
            P("rep", None),
            P("rep", "col"),
            P(("rep", "col"), None),
            P(("rep", "col"), None),
            P(("rep", "col"), None),
        ),
        out_specs=(
            P(("rep", "col"), None),
            P(("rep", "col"), None),
            P(("rep", "col"), None),
            P(("rep", "col"), None),
        ),
        check_vma=False,
    )
```

profile of v0, /device:TPU:0, one launch (start us, length us, event | category | flops | bytes accessed | tf_op | source)
XLA Modules:
  0.0 578.0 jit_solution(5947046217218718542)
XLA Ops:
  0.6 22.6 %fusion.7 = f32[4096,1024]{1,0:T(8,128)S(1)} fusion(bf16[2048,4096]{1,0:T(8,128)(2,1)} %param.5, bf16[2048,1024]{1,0:T(8,128)(2,1)} %param.6), kind=kOutput, calls=%fused_computation.21 | convolution fusion | flops 17179869184 | bytes 37748736 | tf_op jit(solution)/shard_map/td,tc->dc/dot_general | solution.py:39
  23.2 0.0 copy-start
  23.2 4.5 dynamic-slice_bitcast_fusion
  27.7 3.7 copy-done
  31.4 3.1 collective-permute-start
  34.5 180.8 %collective-permute-done = f32[2,1024,1024]{2,1,0:T(8,128)} collective-permute-done((f32[2,1024,1024]{2,1,0:T(8,128)}, f32[2,1024,1024]{2,1,0:T(8,128)}, u32[]{:S(2)}, u32[]{:S(2)}) %collective-permute-start) | collective-permute-done | bytes 8388640 | tf_op jit(solution)/shard_map/ppermute | solution.py:17
  215.2 7.5 %fusion = (f32[]{:T(128)}, f32[]{:T(128)}, f32[]{:T(128)}) fusion(f32[2,2,1024,1024]{3,2,1,0:T(8,128)} %bitcast.36, s32[]{:T(128)S(6)} %select_n.39, f32[2,1024,1024]{2,1,0:T(8,128)} %collective-permute-done), kind=kLoop, calls=%fused_computation.3 | loop fusion | flops 12582909 | bytes 16777232 | tf_op jit(solution)/shard_map/reduce_sum | solution.py:45
  225.4 0.7 pad_maximum_fusion
  226.1 13.0 %psum.14 = f32[3]{0:T(128)S(1)} all-reduce(f32[3]{0:T(128)S(1)} %pad_maximum_fusion), channel_id=1, replica_groups=mesh['rep'=4,'col'=8] {'col'}, use_global_device_ids=true, to_apply=%region_3.4 | all-reduce | flops 3 | bytes 24 | tf_op jit(solution)/shard_map/psum | solution.py:28
  239.1 1.6 collective-permute-start.1
  240.7 2.0 collective-permute-done.1
  242.7 0.6 fusion.6
  247.2 12.1 %fusion.2 = f32[2,1024,1024]{2,1,0:T(8,128)} fusion(f32[2,1024,1024]{2,1,0:T(8,128)} %collective-permute-done, f32[2,2,1024,1024]{3,2,1,0:T(8,128)} %bitcast.37, s32[]{:T(128)S(6)} %select_n.39, f32[]{:T(128)S(6)} %sub.23, f32[]{:T(128)S(6)} %sub.22), kind=kLoop, calls=%fused_computation.5 | loop fusion | flops 6291456 | bytes 25165836 | tf_op jit(solution)/shard_map/add | solution.py:55
  259.2 4.8 constant_dynamic-slice_fusion
  264.0 2.6 collective-permute-start.2
  266.6 178.6 %collective-permute-done.2 = f32[1,1024,1024]{2,1,0:T(8,128)} collective-permute-done((f32[1,1024,1024]{2,1,0:T(8,128)}, f32[1,1024,1024]{2,1,0:T(8,128)}, u32[]{:S(2)}, u32[]{:S(2)}) %collective-permute-start.2) | collective-permute-done | bytes 4194336 | tf_op jit(solution)/shard_map/ppermute | solution.py:17
  445.2 5.2 multiply_reduce_fusion.3
  453.0 0.7 pad_maximum_fusion.1
  453.7 11.8 %psum.15 = f32[3]{0:T(128)S(1)} all-reduce(f32[3]{0:T(128)S(1)} %pad_maximum_fusion.1), channel_id=1, replica_groups=mesh['rep'=4,'col'=8] {'col'}, use_global_device_ids=true, to_apply=%region_7.8 | all-reduce | flops 3 | bytes 24 | tf_op jit(solution)/shard_map/psum | solution.py:28
  465.5 1.4 collective-permute-start.3
  466.9 2.2 collective-permute-done.3
  469.1 2.7 collective-permute-start.4
  471.8 1.8 collective-permute-done.4
  473.6 0.6 fusion.5
  478.1 7.0 %multiply_add_fusion.1 = f32[1,1024,1024]{2,1,0:T(8,128)} fusion(f32[1,1024,1024]{2,1,0:T(8,128)} %collective-permute-done.2, f32[2,1024,1024]{2,1,0:T(8,128)} %fusion.2, s32[]{:T(128)S(6)} %select_n.45, f32[]{:T(128)S(6)} %sub.26, f32[]{:T(128)S(6)} %sub.25), kind=kLoop, calls=%fused_computation.12 | loop fusion | flops 3145728 | bytes 12582924 | tf_op jit(solution)/shard_map/add | solution.py:55
  485.0 4.7 all-to-all-start
  489.8 5.6 copy.11
  495.3 5.6 copy.13
  500.9 5.6 copy.9
  506.5 32.4 %all-to-all-done = f32[8,128,1024]{2,1,0:T(8,128)} async-done(((f32[8,128,1024]{2,1,0:T(8,128)}), f32[8,128,1024]{2,1,0:T(8,128)}, u32[]{:S(2)}, u32[]{:S(2)}) %all-to-all-start) | async-done | bytes 4194336 | tf_op jit(solution)/shard_map/all_to_all | solution.py:64
  538.9 5.3 copy.10
  544.2 11.4 %multiply_subtract_fusion = (f32[128,8192]{0,1:T(8,128)}, f32[128,8192]{0,1:T(8,128)}, f32[128,8192]{0,1:T(8,128)}) fusion(f32[128,8192]{0,1:T(8,128)} %copy.13, f32[128,8,1024]{0,2,1:T(8,128)} %copy.10, f32[128,8192]{0,1:T(8,128)} %copy.9, f32[128,8192]{0,1:T(8,128)} %copy.11), kind=kLoop, calls=%fused_computation.10 | loop fusion | flops 15728640 | bytes 29360128 | tf_op jit(solution)/shard_map/sub | solution.py:68
  555.6 5.6 copy.14
  561.2 5.6 copy.15
  566.8 5.6 copy.16
  572.4 5.6 copy.17
  (3 shorter events, 0.0 us)
Async XLA Ops:
  23.2 8.2 %copy-start = (f32[4096,1024]{1,0:T(8,128)}, f32[4096,1024]{1,0:T(8,128)S(1)}, u32[]{:S(2)}) copy-start(f32[4096,1024]{1,0:T(8,128)S(1)} %fusion.7) | copy-start | bytes 50331652
  31.4 183.8 %collective-permute-start = (f32[2,1024,1024]{2,1,0:T(8,128)}, f32[2,1024,1024]{2,1,0:T(8,128)}, u32[]{:S(2)}, u32[]{:S(2)}) collective-permute-start(f32[2,1024,1024]{2,1,0:T(8,128)} %dynamic-slice_bitcast_fusion), channel_id=1, source_target_pairs={{0,8},{8,0},{16,24},{24,16},{1,9},{9,1},{17,25},{25,17},{2,10},{10... | collective-permute-start | bytes 25165832 | tf_op jit(solution)/shard_map/ppermute | solution.py:17
  239.1 3.6 collective-permute-start.1
  264.0 181.2 %collective-permute-start.2 = (f32[1,1024,1024]{2,1,0:T(8,128)}, f32[1,1024,1024]{2,1,0:T(8,128)}, u32[]{:S(2)}, u32[]{:S(2)}) collective-permute-start(f32[1,1024,1024]{2,1,0:T(8,128)} %constant_dynamic-slice_fusion), channel_id=1, source_target_pairs={{0,16},{16,0},{8,24},{24,8},{1,17},{17,1},{9,25},{25,9},{2,18},{18... | collective-permute-start | bytes 12582920 | tf_op jit(solution)/shard_map/ppermute | solution.py:17
  465.5 3.6 collective-permute-start.3
  469.1 4.5 collective-permute-start.4
  485.0 53.8 %all-to-all-start = ((f32[8,128,1024]{2,1,0:T(8,128)}), f32[8,128,1024]{2,1,0:T(8,128)}, u32[]{:S(2)}, u32[]{:S(2)}) async-start(f32[8,128,1024]{2,1,0:T(8,128)} %bitcast.38), calls=%async_computation | async-start | bytes 8388608 | tf_op jit(solution)/shard_map/all_to_all | solution.py:64
where the time goes:
time: 579 us; the launch traced here: 578 us
  waiting for transfers between devices  398 us (69%)
  local copies, waits for them, and re-layouts  58.6 us (10%)
  other arithmetic  44.6 us (8%)
  blocking collectives  24.7 us (4%)
  matrix products  22.6 us (4%)
  starting transfers between devices  16.1 us (3%)
  between operations  13.7 us (2%)
    ppermute x5, waiting for transfers between devices, swapped(): return lax.ppermute(block, axis, route)  365 us
    unnamed x9, local copies, waits for them, and re-layouts  42.8 us
    all_to_all x1, waiting for transfers between devices, per_device(): lax.all_to_all(reduced, 'col', split_axis=0, concat_axis=1, tiled=True)  32.4 us
    psum x2, blocking collectives, group_total(): total = lax.psum(values, 'col')  24.7 us
    dot_general x1, matrix products, halving_rows(): jnp.einsum('td,tc->dc', acts, cotangent, preferred_element_type=jnp.float32)  22.6 us
    add x2, other arithmetic, halving_rows(): segment = own_coef * own_part + peer_coef * peer_part  19 us
    reduce_sum x2, other arithmetic, halving_rows(): own_sq = jnp.sum(own_part * own_part)  12.7 us
  transfers between devices with their start and end apart: 6, of which 6 were waited for; matrix products, arithmetic and copies ran while one was open for 3% of the time, Pallas kernels for 0%

commit v1 on v0

--- a/solution.py
+++ b/solution.py
@@ -5,6 +5,22 @@
 
 bias_first = 0.9999734386011124
 bias_second = 0.99407947077966
+
+
+def exchange_in_pairs(value, axis, split, join):
+    ways, here = (lax.axis_size(axis), lax.axis_index(axis))
+    width = value.shape[split] // ways
+    dims = list(value.shape)
+    dims[split] = width
+    height = dims[join]
+    dims[join] = height * ways
+    full = jnp.zeros(dims, value.dtype)
+    for mask in range(ways):
+        part = lax.dynamic_slice_in_dim(value, (here ^ mask) * width, width, axis=split)
+        if mask:
+            part = lax.ppermute(part, axis, [(d, d ^ mask) for d in range(ways)])
+        full = lax.dynamic_update_slice_in_dim(full, part, (here ^ mask) * height, axis=join)
+    return full
 
 
 def swapped(block, axis, distance):
@@ -61,7 +77,7 @@
     levels = replicas.bit_length() - 1
     rep_rank = lax.axis_index("rep")
     reduced = halving_rows(acts, cotangent, replicas, levels, rep_rank)
-    combined = lax.all_to_all(reduced, "col", split_axis=0, concat_axis=1, tiled=True)
+    combined = exchange_in_pairs(reduced, "col", 0, 1)
     new_moment = 0.9 * moment + 0.1 * combined
     new_second = 0.95 * second + 0.05 * combined * combined
     update = new_moment / bias_first / (jnp.sqrt(new_second / bias_second) + 1e-08) + 0.1 * weight

time: 579 us -> 542 us (0.936)
  local copies, waits for them, and re-layouts: 58.6 us -> 24.2 us
  other arithmetic: 44.6 us -> 36.6 us
    unnamed x9 -> x12, local copies, waits for them, and re-layouts: 42.8 us -> 5.75 us
    ppermute x0 -> x7, waiting for transfers between devices: none -> 36.8 us  [exchange_in_pairs(): part = lax.ppermute(part, axis, [(d, d ^ mask) for d in range(ways)])]
    all_to_all x1 -> x0, waiting for transfers between devices: 32.4 us -> none  [per_device(): lax.all_to_all(reduced, 'col', split_axis=0, concat_axis=1, tiled=True)]
    dynamic_update_slice x0 -> x8, local copies, waits for them, and re-layouts: none -> 6.53 us  [exchange_in_pairs(): lax.dynamic_update_slice_in_dim(full, part, (here ^ mask) * height, axis=...]
  transfers between devices with their start and end apart: 6 -> 12, of which waited for: 6 -> 8; matrix products, arithmetic and copies ran while one was open for 3% -> 1% of each run, Pallas kernels for 0% -> 0%
where the time goes in v1:
time: 542 us; the launch traced here: 541 us
  waiting for transfers between devices  402 us (74%)
  other arithmetic  36.6 us (7%)
  blocking collectives  24.9 us (5%)
  local copies, waits for them, and re-layouts  24.2 us (4%)
  matrix products  22.6 us (4%)
  starting transfers between devices  16.4 us (3%)
  between operations  13.8 us (3%)
    ppermute x5, waiting for transfers between devices, swapped(): return lax.ppermute(block, axis, route)  365 us
    ppermute x7, waiting for transfers between devices, exchange_in_pairs(): part = lax.ppermute(part, axis, [(d, d ^ mask) for d in range(ways)])  36.8 us
    psum x2, blocking collectives, group_total(): total = lax.psum(values, 'col')  24.9 us
    dot_general x1, matrix products, halving_rows(): jnp.einsum('td,tc->dc', acts, cotangent, preferred_element_type=jnp.float32)  22.6 us
    add x2, other arithmetic, halving_rows(): segment = own_coef * own_part + peer_coef * peer_part  16.5 us
    reduce_sum x2, other arithmetic, halving_rows(): own_sq = jnp.sum(own_part * own_part)  12.7 us
    ppermute x5, starting transfers between devices, swapped(): return lax.ppermute(block, axis, route)  11.4 us
  transfers between devices with their start and end apart: 12, of which 8 were waited for; matrix products, arithmetic and copies ran while one was open for 1% of the time, Pallas kernels for 0%

profile of v1, /device:TPU:0, one launch (start us, length us, event | category | flops | bytes accessed | tf_op | source)
XLA Modules:
  0.0 540.8 jit_solution(6521635939980908042)
XLA Ops:
  0.6 22.6 %fusion.7 = f32[4096,1024]{1,0:T(8,128)S(1)} fusion(bf16[2048,4096]{1,0:T(8,128)(2,1)} %param.5, bf16[2048,1024]{1,0:T(8,128)(2,1)} %param.6), kind=kOutput, calls=%fused_computation.36 | convolution fusion | flops 17179869184 | bytes 37748736 | tf_op jit(solution)/shard_map/td,tc->dc/dot_general | solution.py:55
  23.2 0.0 copy-start
  23.2 4.5 dynamic-slice_bitcast_fusion
  27.7 3.7 copy-done
  31.4 3.1 collective-permute-start
  34.5 180.8 %collective-permute-done = f32[2,1024,1024]{2,1,0:T(8,128)} collective-permute-done((f32[2,1024,1024]{2,1,0:T(8,128)}, f32[2,1024,1024]{2,1,0:T(8,128)}, u32[]{:S(2)}, u32[]{:S(2)}) %collective-permute-start) | collective-permute-done | bytes 8388640 | tf_op jit(solution)/shard_map/ppermute | solution.py:33
  215.2 7.5 %fusion = (f32[]{:T(128)}, f32[]{:T(128)}, f32[]{:T(128)}) fusion(f32[2,2,1024,1024]{3,2,1,0:T(8,128)} %bitcast.44, s32[]{:T(128)S(6)} %select_n.87, f32[2,1024,1024]{2,1,0:T(8,128)} %collective-permute-done), kind=kLoop, calls=%fused_computation.3 | loop fusion | flops 12582909 | bytes 16777232 | tf_op jit(solution)/shard_map/reduce_sum | solution.py:61
  225.4 0.7 pad_maximum_fusion
  226.1 13.0 %psum.14 = f32[3]{0:T(128)S(1)} all-reduce(f32[3]{0:T(128)S(1)} %pad_maximum_fusion), channel_id=1, replica_groups=mesh['rep'=4,'col'=8] {'col'}, use_global_device_ids=true, to_apply=%region_3.4 | all-reduce | flops 3 | bytes 24 | tf_op jit(solution)/shard_map/psum | solution.py:44
  239.1 1.6 collective-permute-start.1
  240.7 2.0 collective-permute-done.1
  242.7 0.6 fusion.6
  247.2 12.1 %fusion.2 = f32[2,1024,1024]{2,1,0:T(8,128)} fusion(f32[2,1024,1024]{2,1,0:T(8,128)} %collective-permute-done, f32[2,2,1024,1024]{3,2,1,0:T(8,128)} %bitcast.45, s32[]{:T(128)S(6)} %select_n.87, f32[]{:T(128)S(6)} %sub.23, f32[]{:T(128)S(6)} %sub.22), kind=kLoop, calls=%fused_computation.5 | loop fusion | flops 6291456 | bytes 25165836 | tf_op jit(solution)/shard_map/add | solution.py:71
  259.2 4.8 constant_dynamic-slice_fusion
  264.0 2.6 collective-permute-start.2
  266.6 178.6 %collective-permute-done.2 = f32[1,1024,1024]{2,1,0:T(8,128)} collective-permute-done((f32[1,1024,1024]{2,1,0:T(8,128)}, f32[1,1024,1024]{2,1,0:T(8,128)}, u32[]{:S(2)}, u32[]{:S(2)}) %collective-permute-start.2) | collective-permute-done | bytes 4194336 | tf_op jit(solution)/shard_map/ppermute | solution.py:33
  445.2 5.2 multiply_reduce_fusion.3
  453.0 0.7 pad_maximum_fusion.1
  453.7 12.0 %psum.15 = f32[3]{0:T(128)S(1)} all-reduce(f32[3]{0:T(128)S(1)} %pad_maximum_fusion.1), channel_id=1, replica_groups=mesh['rep'=4,'col'=8] {'col'}, use_global_device_ids=true, to_apply=%region_7.8 | all-reduce | flops 3 | bytes 24 | tf_op jit(solution)/shard_map/psum | solution.py:44
  465.7 1.4 collective-permute-start.3
  467.1 2.2 collective-permute-done.3
  469.3 2.7 collective-permute-start.4
  472.0 1.8 collective-permute-done.4
  473.8 0.6 fusion.5
  478.3 4.5 multiply_add_fusion.1
  482.7 0.0 copy-start.2
  482.7 2.0 copy-done.2
  484.7 1.1 dynamic-slice_bitcast_fusion.1
  485.8 0.0 collective-permute-start.5
  485.8 0.0 collective-permute-start.6
  485.8 1.9 collective-permute-start.7
  487.7 1.6 collective-permute-start.8
  489.2 0.0 collective-permute-start.9
  489.3 0.0 copy-start.5
  489.3 0.4 broadcast_in_dim.3
  489.7 0.0 copy-start.3
  489.7 0.0 copy-start.4
  489.7 1.3 bitcast_dynamic-update-slice_fusion
  491.0 0.0 collective-permute-done.5
  491.0 1.2 collective-permute-start.10
  492.3 1.8 constant_dynamic-update-slice_fusion.6
  494.1 6.6 %collective-permute-done.6 = f32[128,1024]{1,0:T(8,128)} collective-permute-done((f32[128,1024]{1,0:T(8,128)S(1)}, f32[128,1024]{1,0:T(8,128)}, u32[]{:S(2)}, u32[]{:S(2)}) %collective-permute-start.6) | collective-permute-done | bytes 524320 | tf_op jit(solution)/shard_map/ppermute | solution.py:21
  500.7 0.4 collective-permute-start.11
  501.1 1.1 constant_dynamic-update-slice_fusion.5
  502.2 8.8 %collective-permute-done.7 = f32[128,1024]{1,0:T(8,128)} collective-permute-done((f32[128,1024]{1,0:T(8,128)S(1)}, f32[128,1024]{1,0:T(8,128)}, u32[]{:S(2)}, u32[]{:S(2)}) %collective-permute-start.7) | collective-permute-done | bytes 524320 | tf_op jit(solution)/shard_map/ppermute | solution.py:21
  511.0 1.1 constant_dynamic-update-slice_fusion.4
  512.1 0.0 collective-permute-done.8
  512.1 1.1 constant_dynamic-update-slice_fusion.3
  513.2 21.4 %collective-permute-done.9 = f32[128,1024]{1,0:T(8,128)S(1)} collective-permute-done((f32[128,1024]{1,0:T(8,128)S(1)}, f32[128,1024]{1,0:T(8,128)S(1)}, u32[]{:S(2)}, u32[]{:S(2)}) %collective-permute-start.9) | collective-permute-done | bytes 524320 | tf_op jit(solution)/shard_map/ppermute | solution.py:21
  534.6 0.0 collective-permute-done.10
  534.7 0.1 constant_dynamic-update-slice_fusion.1
  534.7 0.0 collective-permute-done.11
  534.7 0.1 constant_dynamic-update-slice_fusion
  534.8 0.0 copy-done.5
  534.8 0.0 copy-done.3
  534.8 0.0 copy-done.4
  534.8 0.0 copy-start.1
  534.8 6.0 %multiply_subtract_fusion = (f32[128,8192]{1,0:T(8,128)}, f32[128,8192]{1,0:T(8,128)}, f32[128,8192]{1,0:T(8,128)}) fusion(f32[128,8192]{1,0:T(8,128)S(1)} %copy-done.3, f32[128,8192]{1,0:T(8,128)S(1)} %constant_dynamic-update-slice_fusion, f32[128,8192]{1,0:T(8,128)S(1)} %copy-done.4, f32[128,8192]{1,0:T(8,128)S(1)} %copy-done.5), kind=kLoop, calls=%fused_computation.10 | loop fusion | flops 15728640 | bytes 29360128 | tf_op jit(solution)/shard_map/sub | solution.py:84
  540.8 0.0 copy-done.1
  (4 shorter events, 0.1 us)
Async XLA Ops:
  23.2 8.2 %copy-start = (f32[4096,1024]{1,0:T(8,128)}, f32[4096,1024]{1,0:T(8,128)S(1)}, u32[]{:S(2)}) copy-start(f32[4096,1024]{1,0:T(8,128)S(1)} %fusion.7) | copy-start | bytes 50331652
  31.4 183.8 %collective-permute-start = (f32[2,1024,1024]{2,1,0:T(8,128)}, f32[2,1024,1024]{2,1,0:T(8,128)}, u32[]{:S(2)}, u32[]{:S(2)}) collective-permute-start(f32[2,1024,1024]{2,1,0:T(8,128)} %dynamic-slice_bitcast_fusion), channel_id=1, source_target_pairs={{0,8},{8,0},{16,24},{24,16},{1,9},{9,1},{17,25},{25,17},{2,10},{10... | collective-permute-start | bytes 25165832 | tf_op jit(solution)/shard_map/ppermute | solution.py:33
  239.1 3.6 collective-permute-start.1
  264.0 181.2 %collective-permute-start.2 = (f32[1,1024,1024]{2,1,0:T(8,128)}, f32[1,1024,1024]{2,1,0:T(8,128)}, u32[]{:S(2)}, u32[]{:S(2)}) collective-permute-start(f32[1,1024,1024]{2,1,0:T(8,128)} %constant_dynamic-slice_fusion), channel_id=1, source_target_pairs={{0,16},{16,0},{8,24},{24,8},{1,17},{17,1},{9,25},{25,9},{2,18},{18... | collective-permute-start | bytes 12582920 | tf_op jit(solution)/shard_map/ppermute | solution.py:33
  465.7 3.6 collective-permute-start.3
  469.3 4.5 collective-permute-start.4
  482.7 2.0 copy-start.2
  485.8 5.2 collective-permute-start.5
  485.8 14.9 %collective-permute-start.6 = (f32[128,1024]{1,0:T(8,128)S(1)}, f32[128,1024]{1,0:T(8,128)}, u32[]{:S(2)}, u32[]{:S(2)}) collective-permute-start(f32[128,1024]{1,0:T(8,128)S(1)} %get-tuple-element.18), channel_id=1, source_target_pairs={{0,2},{1,3},{2,0},{3,1},{4,6},{5,7},{6,4},{7,5},{8,10},{9,11},{10,... | collective-permute-start | bytes 1572872 | tf_op jit(solution)/shard_map/ppermute | solution.py:21
  485.8 25.2 %collective-permute-start.7 = (f32[128,1024]{1,0:T(8,128)S(1)}, f32[128,1024]{1,0:T(8,128)}, u32[]{:S(2)}, u32[]{:S(2)}) collective-permute-start(f32[128,1024]{1,0:T(8,128)S(1)} %get-tuple-element.17), channel_id=1, source_target_pairs={{0,3},{1,2},{2,1},{3,0},{4,7},{5,6},{6,5},{7,4},{8,11},{9,10},{10,... | collective-permute-start | bytes 1572872 | tf_op jit(solution)/shard_map/ppermute | solution.py:21
  487.7 24.4 %collective-permute-start.8 = (f32[128,1024]{1,0:T(8,128)S(1)}, f32[128,1024]{1,0:T(8,128)}, u32[]{:S(2)}, u32[]{:S(2)}) collective-permute-start(f32[128,1024]{1,0:T(8,128)S(1)} %get-tuple-element.16), channel_id=1, source_target_pairs={{0,4},{1,5},{2,6},{3,7},{4,0},{5,1},{6,2},{7,3},{8,12},{9,13},{10,... | collective-permute-start | bytes 1572872 | tf_op jit(solution)/shard_map/ppermute | solution.py:21
  489.2 45.3 %collective-permute-start.9 = (f32[128,1024]{1,0:T(8,128)S(1)}, f32[128,1024]{1,0:T(8,128)S(1)}, u32[]{:S(2)}, u32[]{:S(2)}) collective-permute-start(f32[128,1024]{1,0:T(8,128)S(1)} %get-tuple-element.15), channel_id=1, source_target_pairs={{0,5},{1,4},{2,7},{3,6},{4,1},{5,0},{6,3},{7,2},{8,13},{9,12},{10,... | collective-permute-start | bytes 1572872 | tf_op jit(solution)/shard_map/ppermute | solution.py:21
  489.3 45.5 %copy-start.5 = (f32[128,8192]{1,0:T(8,128)S(1)}, f32[128,8192]{1,0:T(8,128)}, u32[]{:S(2)}) copy-start(f32[128,8192]{1,0:T(8,128)} %param.9) | copy-start | bytes 12582916
  489.7 45.1 %copy-start.3 = (f32[128,8192]{1,0:T(8,128)S(1)}, f32[128,8192]{1,0:T(8,128)}, u32[]{:S(2)}) copy-start(f32[128,8192]{1,0:T(8,128)} %param.7) | copy-start | bytes 12582916
  489.7 45.1 %copy-start.4 = (f32[128,8192]{1,0:T(8,128)S(1)}, f32[128,8192]{1,0:T(8,128)}, u32[]{:S(2)}) copy-start(f32[128,8192]{1,0:T(8,128)} %param.8) | copy-start | bytes 12582916
  491.0 43.6 %collective-permute-start.10 = (f32[128,1024]{1,0:T(8,128)S(1)}, f32[128,1024]{1,0:T(8,128)S(1)}, u32[]{:S(2)}, u32[]{:S(2)}) collective-permute-start(f32[128,1024]{1,0:T(8,128)S(1)} %get-tuple-element.14), channel_id=1, source_target_pairs={{0,6},{1,7},{2,4},{3,5},{4,2},{5,3},{6,0},{7,1},{8,14},{9,15},{10,... | collective-permute-start | bytes 1572872 | tf_op jit(solution)/shard_map/ppermute | solution.py:21
  500.7 34.0 %collective-permute-start.11 = (f32[128,1024]{1,0:T(8,128)S(1)}, f32[128,1024]{1,0:T(8,128)S(1)}, u32[]{:S(2)}, u32[]{:S(2)}) collective-permute-start(f32[128,1024]{1,0:T(8,128)S(1)} %get-tuple-element.13), channel_id=1, source_target_pairs={{0,7},{1,6},{2,5},{3,4},{4,3},{5,2},{6,1},{7,0},{8,15},{9,14},{10,... | collective-permute-start | bytes 1572872 | tf_op jit(solution)/shard_map/ppermute | solution.py:21
  534.8 6.0 %copy-start.1 = (f32[128,8192]{1,0:T(8,128)}, f32[128,8192]{1,0:T(8,128)S(1)}, u32[]{:S(2)}) copy-start(f32[128,8192]{1,0:T(8,128)S(1)} %constant_dynamic-update-slice_fusion) | copy-start | bytes 12582916
